TPU v7x, 256 devices: a whole 4x4x8 slice. The times are simulated.
256 devices in a mesh: row: 16 (over z, y_lo), col: 16 (over y_hi, x, core).
Axes of the slice: x: 4, y: 4 (y_hi: 2, y_lo: 2; y = y_hi * 2 + y_lo), z: 8, core: 2. Of those that a mesh axis runs over, the one named last changes fastest.
Arguments:
- ancestor: float32 [8192, 8192], P('row', 'col'), may hold values from -0.0625 to 0.0625
- factor: float32 [8192, 16, 128], P(('row', 'col')), may hold values from -1.5 to 1.5
- diag_inv: float32 [16, 128, 128], replicated, may hold values from -6 to 6
- structure: int32 [16, 768], replicated, may hold values from 0 to 1023, as said below
Outputs:
- inverse_panel: float32 [8192, 16, 128], P(('row', 'col'))
- inverse_diagonal: float32 [16, 128, 128], replicated
Inputs may be any that keep to these rules, and one draw needn't show every extreme that they name: Each row of structure lists 768 different block numbers, in no particular order.
All inputs are finite; a program needn't handle non-finite values.
Results may differ from a plain program's by a relative error of at most 0.00007.
Values sent between devices are 32-bit elements; how exact they have to be, the bound alone decides.
No kernel may reach another device: no remote copies, remote signals or barrier semaphores. Data moves between devices by JAX's collectives and lax.ppermute only.
A program may use at most 64 MiB of HBM per device.

v0:
```python
import jax
import jax.numpy as jnp
from jax import lax
from jax.sharding import PartitionSpec as P

RB = 8


def spread_2(value, axis, source):
    kept = jnp.where(lax.axis_index(axis) == source, value, 0).astype(value.dtype)
    return lax.psum(kept, axis)


def per_device(ancestor, factor, diag_inv, structure):
    row_devices = lax.axis_size("row")
    col_devices = lax.axis_size("col")
    ratio = row_devices // col_devices
    local_rows = factor.shape[0]
    width = factor.shape[2]
    first_row = (lax.axis_index("row") * col_devices + lax.axis_index("col")) * local_rows
    block_ids = (first_row + jnp.arange(local_rows, dtype=jnp.int32)) // RB
    matches = block_ids[:, None, None] == structure[None, :, :]
    row_mask = jnp.any(matches, axis=2).astype(jnp.float32)
    masked = factor * row_mask[:, :, None]
    count_sib = masked.shape[1]
    spread = masked.reshape(local_rows, count_sib * width)
    block_row = lax.all_gather(spread, "col", axis=0, tiled=True)
    received = spread_2(block_row, "row", lax.axis_index("col") * ratio + 0)
    summed = lax.psum_scatter(
        jnp.dot(
            ancestor, received, precision=lax.Precision.HIGHEST, preferred_element_type=jnp.float32
        ),
        "col",
        scatter_dimension=0,
        tiled=True,
    )
    panel = -summed.reshape(local_rows, count_sib, width)
    panel = panel * row_mask[:, :, None]
    local_update = jnp.einsum("bsw,bsv->swv", masked, panel, precision=lax.Precision.HIGHEST)
    total_update = lax.psum(local_update, ("row", "col"))
    return (panel, diag_inv - total_update)


def solution(mesh):
    placed = (P("row", "col"), P(("row", "col"), None, None), P(), P())
    return jax.shard_map(
        per_device,
        mesh=mesh,
        in_specs=placed,
        out_specs=(P(("row", "col"), None, None), P()),
        check_vma=False,
    )
```

profile of v0, /device:TPU:2, one launch (start us, length us, event | category | flops | bytes accessed | tf_op | source)
XLA Modules:
  0.0 657.8 jit_solution(703054387542532473)
XLA Ops:
  7.2 0.0 copy-start
  7.2 0.0 all-gather.2.cloned.1.call-start
  7.2 1.6 compare_reduce_fusion
  8.8 1.1 broadcast_multiply_fusion.1
  9.9 0.8 copy.23
  10.7 0.0 all-gather.2.cloned.1.call-update
  10.7 0.0 all-reduce.3.cloned.1.call-start
  10.8 64.4 %all-gather.2.cloned.1.call-done = f32[512,2048]{1,0:T(8,128)} async-done(((f32[32,2048]{1,0:T(8,128)}), f32[512,2048]{1,0:T(8,128)}) %all-gather.2.cloned.1.call-update) | async-done | bytes 4194320 | tf_op jit(solution)/shard_map/all_gather | solution.py:27
  75.2 2.5 broadcast_select_fusion
  77.7 0.0 all-reduce.3.cloned.1.call-update
  77.7 0.0 reduce-scatter.4.cloned.1.call-start
  77.8 199.0 %all-reduce.3.cloned.1.call-done = f32[512,2048]{1,0:T(8,128)} async-done(((f32[512,2048]{1,0:T(8,128)}), f32[512,2048]{1,0:T(8,128)}) %all-reduce.3.cloned.1.call-update) | async-done | bytes 4194320 | tf_op jit(solution)/shard_map/psum | solution.py:11
  276.8 0.0 copy-done
  276.8 16.3 %convolution_bitcast_fusion = f32[512,2048]{0,1:T(8,128)} fusion(f32[512,2048]{1,0:T(8,128)} %all-reduce.3.cloned.1.call-done, f32[512,512]{1,0:T(8,128)S(1)} %copy-done), kind=kOutput, calls=%fused_computation | convolution fusion | flops 6442450944 | bytes 9437184 | tf_op jit(solution)/shard_map/dot_general | solution.py:30
  293.0 5.4 copy.15
  298.4 0.0 reduce-scatter.4.cloned.1.call-update
  298.5 0.0 all-reduce.5.cloned.1.call-start
  298.5 88.3 %reduce-scatter.4.cloned.1.call-done = f32[32,2048]{1,0:T(8,128)} async-done(((f32[512,2048]{1,0:T(8,128)}), f32[32,2048]{1,0:T(8,128)}) %reduce-scatter.4.cloned.1.call-update) | async-done | bytes 262160
  386.8 1.3 copy.16
  388.1 0.1 neg.6
  388.2 0.3 copy.12
  388.5 0.1 broadcast_multiply_fusion
  388.7 0.0 copy-start.1
  388.7 2.8 fusion
  391.5 0.0 all-reduce.5.cloned.1.call-update
  391.5 257.1 %all-reduce.5.cloned.1.call-done = f32[16,128,128]{2,1,0:T(8,128)} async-done(((f32[16,128,128]{2,1,0:T(8,128)}), f32[16,128,128]{2,1,0:T(8,128)}) %all-reduce.5.cloned.1.call-update) | async-done | bytes 1048592 | tf_op jit(solution)/shard_map/psum | solution.py:40
  648.6 2.6 sub.10
  651.3 0.0 copy-done.1
  (2 shorter events, 0.0 us)
Async XLA Ops:
  7.2 269.6 %copy-start = (f32[512,512]{1,0:T(8,128)S(1)}, f32[512,512]{1,0:T(8,128)}, u32[]{:S(2)}) copy-start(f32[512,512]{1,0:T(8,128)} %param.4) | copy-start | bytes 3145732
  7.2 68.0 %all-gather.2.cloned.1.call-start = ((), (), s32[]{:S(2)}) async-start(), calls=%async_computation.1 | async-start | bytes 4456448 | tf_op jit(solution)/shard_map/all_gather | solution.py:27
  10.7 266.0 %all-reduce.3.cloned.1.call-start = ((), (), s32[]{:S(2)}) async-start(), calls=%async_computation.2 | async-start | bytes 8388608 | tf_op jit(solution)/shard_map/psum | solution.py:11
  77.7 309.1 %reduce-scatter.4.cloned.1.call-start = ((), (), s32[]{:S(2)}) async-start(), calls=%async_computation.4 | async-start | bytes 4456448
  298.5 350.2 %all-reduce.5.cloned.1.call-start = ((), (), s32[]{:S(2)}) async-start(), calls=%async_computation.3 | async-start | bytes 2097152 | tf_op jit(solution)/shard_map/psum | solution.py:40
  388.7 262.6 %copy-start.1 = (f32[32,16,128]{2,1,0:T(8,128)}, f32[32,16,128]{2,1,0:T(8,128)S(1)}, u32[]{:S(2)}) copy-start(f32[32,16,128]{2,1,0:T(8,128)S(1)} %broadcast_multiply_fusion) | copy-start | bytes 786436
Sparse Core Ops, SparseCore 0:
  11.3 63.8 all-gather.1
  77.8 198.8 all-reduce.2
  298.6 88.2 reduce-scatter.3
  393.6 254.9 all-reduce.4
where the time goes:
time: 658 us
  waiting for transfers between devices  609 us (93%)
  matrix products  19.1 us (3%)
  between operations  13.8 us (2%)
  other arithmetic  8.03 us (1%)
  local copies, waits for them, and re-layouts  7.8 us (1%)
    psum x1, waiting for transfers between devices, per_device(): total_update = lax.psum(local_update, ('row', 'col'))  257 us
    psum x1, waiting for transfers between devices, spread_2(): return lax.psum(kept, axis)  199 us
    unnamed x5, waiting for transfers between devices  88.4 us
    all_gather x1, waiting for transfers between devices, per_device(): block_row = lax.all_gather(spread, 'col', axis=0, tiled=True)  64.4 us
    dot_general x1, matrix products, per_device(): jnp.dot(ancestor, received, precision=lax.Precision.HIGHEST, preferred_el...  16.3 us
  transfers between devices with their start and end apart: 4, of which 4 were waited for; matrix products, arithmetic and copies ran while one was open for 0% of the time, Pallas kernels for 0%

commit v1 on v0

--- a/solution.py
+++ b/solution.py
@@ -1,9 +1,19 @@
+import functools
 import jax
 import jax.numpy as jnp
 from jax import lax
 from jax.sharding import PartitionSpec as P
 
 RB = 8
+
+
+def form_things(incoming_x, dim_i):
+    everything = jnp.stack([incoming_x for _ in range(lax.axis_size("col"))], axis=0)
+    far_arr = lax.all_to_all(everything, "col", 0, 0)
+    return jnp.concatenate(far_arr, dim_i)
+
+
+register_vector = functools.partial(form_things, dim_i=0)
 
 
 def spread_2(value, axis, source):
@@ -24,7 +34,7 @@
     masked = factor * row_mask[:, :, None]
     count_sib = masked.shape[1]
     spread = masked.reshape(local_rows, count_sib * width)
-    block_row = lax.all_gather(spread, "col", axis=0, tiled=True)
+    block_row = register_vector(spread)
     received = spread_2(block_row, "row", lax.axis_index("col") * ratio + 0)
     summed = lax.psum_scatter(
         jnp.dot(

time: 658 us -> 663 us (level)
  starting transfers between devices: 0.16 us -> 7.6 us
    all_gather x1 -> x0, waiting for transfers between devices: 64.4 us -> none  [per_device(): block_row = lax.all_gather(spread, 'col', axis=0, tiled=True)]
    all_to_all x0 -> x1, waiting for transfers between devices: none -> 56.9 us  [form_things(): far_arr = lax.all_to_all(everything, 'col', 0, 0)]
    all_to_all x0 -> x1, starting transfers between devices: none -> 7.48 us  [form_things(): far_arr = lax.all_to_all(everything, 'col', 0, 0)]
    unnamed x5 -> x4, waiting for transfers between devices: 88.4 us -> 88.4 us
where the time goes in v1:
time: 663 us
  waiting for transfers between devices  605 us (91%)
  matrix products  19.1 us (3%)
  between operations  13.8 us (2%)
  local copies, waits for them, and re-layouts  9.63 us (1%)
  other arithmetic  8.03 us (1%)
  starting transfers between devices  7.6 us (1%)
    psum x1, waiting for transfers between devices, per_device(): total_update = lax.psum(local_update, ('row', 'col'))  257 us
    psum x1, waiting for transfers between devices, spread_2(): return lax.psum(kept, axis)  202 us
    unnamed x4, waiting for transfers between devices  88.4 us
    all_to_all x1, waiting for transfers between devices, form_things(): far_arr = lax.all_to_all(everything, 'col', 0, 0)  56.9 us
    dot_general x1, matrix products, per_device(): jnp.dot(ancestor, received, precision=lax.Precision.HIGHEST, preferred_el...  16.3 us
  transfers between devices with their start and end apart: 4, of which 4 were waited for; matrix products, arithmetic and copies ran while one was open for 0% of the time, Pallas kernels for 0%

profile of v1, /device:TPU:2, one launch (start us, length us, event | category | flops | bytes accessed | tf_op | source)
XLA Modules:
  0.0 662.8 jit_solution(6437672387634224250)
XLA Ops:
  7.2 0.0 copy-start
  7.2 1.6 compare_reduce_fusion
  8.8 1.1 broadcast_multiply_fusion.1
  9.9 0.1 copy.23
  10.0 2.5 stack.3
  12.4 7.5 %all-to-all-start = ((f32[16,32,2048]{2,1,0:T(8,128)}), f32[16,32,2048]{2,1,0:T(8,128)}, u32[]{:S(2)}, u32[]{:S(2)}) async-start(f32[16,32,2048]{2,1,0:T(8,128)} %stack.3), calls=%async_computation | async-start | bytes 8388608 | tf_op jit(solution)/shard_map/all_to_all | solution.py:12
  19.9 0.0 all-reduce.3.cloned.1.call-start
  20.0 56.9 %all-to-all-done = f32[16,32,2048]{2,1,0:T(8,128)} async-done(((f32[16,32,2048]{2,1,0:T(8,128)}), f32[16,32,2048]{2,1,0:T(8,128)}, u32[]{:S(2)}, u32[]{:S(2)}) %all-to-all-start) | async-done | bytes 4194336 | tf_op jit(solution)/shard_map/all_to_all | solution.py:12
  76.9 2.5 broadcast_select_fusion
  79.4 0.0 all-reduce.3.cloned.1.call-update
  79.4 0.0 reduce-scatter.4.cloned.1.call-start
  79.5 202.0 %all-reduce.3.cloned.1.call-done = f32[512,2048]{1,0:T(8,128)} async-done(((f32[512,2048]{1,0:T(8,128)}), f32[512,2048]{1,0:T(8,128)}) %all-reduce.3.cloned.1.call-update) | async-done | bytes 4194320 | tf_op jit(solution)/shard_map/psum | solution.py:21
  281.5 0.0 copy-done
  281.5 16.3 %convolution_bitcast_fusion = f32[512,2048]{0,1:T(8,128)} fusion(f32[512,2048]{1,0:T(8,128)} %all-reduce.3.cloned.1.call-done, f32[512,512]{1,0:T(8,128)S(1)} %copy-done), kind=kOutput, calls=%fused_computation | convolution fusion | flops 6442450944 | bytes 9437184 | tf_op jit(solution)/shard_map/dot_general | solution.py:40
  297.8 5.5 copy.15
  303.2 0.0 reduce-scatter.4.cloned.1.call-update
  303.2 0.0 all-reduce.5.cloned.1.call-start
  303.3 88.4 %reduce-scatter.4.cloned.1.call-done = f32[32,2048]{1,0:T(8,128)} async-done(((f32[512,2048]{1,0:T(8,128)}), f32[32,2048]{1,0:T(8,128)}) %reduce-scatter.4.cloned.1.call-update) | async-done | bytes 262160
  391.7 1.3 copy.16
  393.0 0.1 neg.6
  393.0 0.3 copy.12
  393.4 0.1 broadcast_multiply_fusion
  393.5 0.0 copy-start.1
  393.5 2.8 fusion
  396.3 0.0 all-reduce.5.cloned.1.call-update
  396.3 257.3 %all-reduce.5.cloned.1.call-done = f32[16,128,128]{2,1,0:T(8,128)} async-done(((f32[16,128,128]{2,1,0:T(8,128)}), f32[16,128,128]{2,1,0:T(8,128)}) %all-reduce.5.cloned.1.call-update) | async-done | bytes 1048592 | tf_op jit(solution)/shard_map/psum | solution.py:50
  653.6 2.6 sub.10
  656.3 0.0 copy-done.1
  (2 shorter events, 0.0 us)
Async XLA Ops:
  7.2 274.3 %copy-start = (f32[512,512]{1,0:T(8,128)S(1)}, f32[512,512]{1,0:T(8,128)}, u32[]{:S(2)}) copy-start(f32[512,512]{1,0:T(8,128)} %param.4) | copy-start | bytes 3145732
  12.4 64.4 %all-to-all-start = ((f32[16,32,2048]{2,1,0:T(8,128)}), f32[16,32,2048]{2,1,0:T(8,128)}, u32[]{:S(2)}, u32[]{:S(2)}) async-start(f32[16,32,2048]{2,1,0:T(8,128)} %stack.3), calls=%async_computation | async-start | bytes 8388608 | tf_op jit(solution)/shard_map/all_to_all | solution.py:12
  19.9 261.6 %all-reduce.3.cloned.1.call-start = ((), (), s32[]{:S(2)}) async-start(), calls=%async_computation.2 | async-start | bytes 8388608 | tf_op jit(solution)/shard_map/psum | solution.py:21
  79.4 312.3 %reduce-scatter.4.cloned.1.call-start = ((), (), s32[]{:S(2)}) async-start(), calls=%async_computation.4 | async-start | bytes 4456448
  303.2 350.4 %all-reduce.5.cloned.1.call-start = ((), (), s32[]{:S(2)}) async-start(), calls=%async_computation.3 | async-start | bytes 2097152 | tf_op jit(solution)/shard_map/psum | solution.py:50
  393.5 262.8 %copy-start.1 = (f32[32,16,128]{2,1,0:T(8,128)}, f32[32,16,128]{2,1,0:T(8,128)S(1)}, u32[]{:S(2)}) copy-start(f32[32,16,128]{2,1,0:T(8,128)S(1)} %broadcast_multiply_fusion) | copy-start | bytes 786436
Sparse Core Ops, SparseCore 0:
  79.5 201.9 all-reduce.2
  303.4 88.2 reduce-scatter.3
  398.6 254.9 all-reduce.4
